TPU v7x, 512 devices: a whole 4x8x8 slice. The times are simulated.
512 devices in a mesh: row: 16 (over z, y_lo), col: 32 (over x, y_hi, core).
Axes of the slice: x: 4, y: 8 (y_hi: 4, y_lo: 2; y = y_hi * 2 + y_lo), z: 8, core: 2. Of those that a mesh axis runs over, the one named last changes fastest.
Arguments:
- features: bfloat16 [65536, 128], P(('col', 'row')), may hold values from -6 to 6
- grad_out: bfloat16 [65536, 128], P(('row', 'col')), may hold values from -6 to 6
- weight: bfloat16 [128, 128], replicated, may hold values from -0.5 to 0.5
- block_ids: int32 [16, 32, 152], P('row', 'col'), may hold values from 0 to 511, as said below
- block_vals: bfloat16 [16, 32, 152, 128, 128], P('row', 'col'), may hold values from -0.0390625 to 0.0390625
- block_count: int32 [16, 32], P('row', 'col'), may hold values from 1 to 152
- node_perm: int32 [512, 128], P(('col', 'row')), may hold values from 0 to 127, each once within a row
Outputs:
- feature_grad: bfloat16 [65536, 128], P(('col', 'row'))
- weight_grad: float32 [128, 128], replicated
Inputs may be any that keep to these rules, and one draw needn't show every extreme that they name: `block_ids`: in each tile the 152 entries are distinct block positions p * 16 + q; slots at or beyond block_count are empty and must be ignored. `node_perm`: each row is a permutation of 0 to 127.
All inputs are finite; a program needn't handle non-finite values.
Results may differ from a plain program's by a relative error of at most 0.0059.
Values may be sent and summed in bfloat16 or wider, within the bound.
A program may use at most 128 MiB of HBM per device.

v0:
```python
import math
import jax
import jax.numpy as jnp
from jax import lax
from jax.sharding import PartitionSpec as P

BLOCK = 128


def grad_step(agg_low, grad_rows, weight):
    pre = jnp.dot(agg_low, weight, preferred_element_type=jnp.float32)
    sigma = jax.nn.sigmoid(pre)
    grad_pre = (grad_rows.astype(jnp.float32) * sigma * (1.0 + pre * (1.0 - sigma))).astype(
        jnp.bfloat16
    )
    grad_agg = lax.dot_general(
        grad_pre, weight, (((1,), (1,)), ((), ())), preferred_element_type=jnp.float32
    )
    return (grad_pre, grad_agg.astype(jnp.bfloat16))


def block_sums(product, targets, live, segments):
    routed = jnp.where(live, targets, segments)
    summed = jax.ops.segment_sum(product, routed, num_segments=segments + 1)
    return summed[:segments]


def shards(features, grad_out, weight, block_ids, block_vals, block_count, node_perm):
    nodes_dev = grad_out.shape[0]
    hidden = weight.shape[0]
    tile_ids = block_ids[0, 0]
    values = block_vals[0, 0]
    count_live = block_count[0, 0]
    slots_tile = tile_ids.shape[0]
    row_count = nodes_dev * lax.axis_size("col") // BLOCK
    col_count = nodes_dev * lax.axis_size("row") // BLOCK
    total_nodes = nodes_dev * lax.axis_size("row") * lax.axis_size("col")
    live = jnp.arange(slots_tile, dtype=jnp.int32) < count_live
    block_row = tile_ids // col_count
    block_col = tile_ids % col_count
    column_source = lax.all_gather(features, "row", axis=0, tiled=True)
    picked = column_source.reshape(col_count, BLOCK, hidden)[block_col]
    product = jnp.einsum("kij,kjf->kif", values, picked, preferred_element_type=jnp.float32)
    partial_value = block_sums(product, block_row, live, row_count).reshape(
        row_count * BLOCK, hidden
    )
    aggregate = lax.psum_scatter(partial_value, "col", scatter_dimension=0, tiled=True)
    agg_low = aggregate.astype(jnp.bfloat16)
    grad_pre, grad_share = grad_step(agg_low, grad_out, weight)
    weight_part = jnp.dot(agg_low.T, grad_pre, preferred_element_type=jnp.float32)
    grad_rows = lax.all_gather(grad_share, "col", axis=0, tiled=True)
    weight_grad = lax.psum(weight_part, ("row", "col")) * (1.0 / math.sqrt(total_nodes))
    picked_back = grad_rows.reshape(row_count, BLOCK, hidden)[block_row]
    product_back = jnp.einsum(
        "kij,kif->kjf", values, picked_back, preferred_element_type=jnp.float32
    )
    partial_back = block_sums(product_back, block_col, live, col_count).reshape(
        col_count * BLOCK, hidden
    )
    grad_share_cols = lax.psum_scatter(partial_back, "row", scatter_dimension=0, tiled=True)
    rounded = grad_share_cols.astype(jnp.bfloat16)
    feature_grad = rounded[node_perm[0]]
    return (feature_grad, weight_grad)


def solution(mesh):
    in_specs = (
        P(("col", "row"), None),
        P(("row", "col"), None),
        P(),
        P("row", "col", None),
        P("row", "col", None, None, None),
        P("row", "col"),
        P(("col", "row"), None),
    )
    out_specs = (P(("col", "row"), None), P())
    return jax.shard_map(shards, mesh=mesh, in_specs=in_specs, out_specs=out_specs, check_vma=False)
```

profile of v0, /device:TPU:4, one launch (start us, length us, event | category | flops | bytes accessed | tf_op | source)
XLA Modules:
  0.0 607.2 jit_solution(2033896433721760579)
XLA Ops:
  7.2 0.7 compare_select_fusion
  8.6 44.5 %all_gather.6 = bf16[2048,128]{1,0:T(8,128)(2,1)S(1)} all-gather(bf16[128,128]{1,0:T(8,128)(2,1)} %param.7), channel_id=1, replica_groups=mesh['row'=16,'col'=32] {'row'}, dimensions={0}, use_global_device_ids=true | all-gather | bytes 557056 | tf_op jit(solution)/shard_map/all_gather | solution.py:41
  53.1 7.7 %gather_fusion = bf16[152,128,128]{2,1,0:T(8,128)(2,1)} fusion(bf16[16,128,128]{2,1,0:T(8,128)(2,1)S(1)} %bitcast.46, s32[1024]{0:T(1024)S(1)} %pad_clamp_fusion.2), kind=kCustom, calls=%fused_computation | custom fusion | bytes 9962080 | tf_op jit(solution)/shard_map/gather | solution.py:42
  60.8 11.3 %fusion.4 = f32[152,128,128]{1,2,0:T(8,128)} fusion(bf16[152,128,128]{2,1,0:T(8,128)(2,1)} %gather_fusion, bf16[1,1,152,128,128]{4,3,2,1,0:T(8,128)(2,1)} %param.11), kind=kOutput, calls=%fused_computation.9 | convolution fusion | flops 637534208 | bytes 19922944 | tf_op jit(solution)/shard_map/kij,kjf->kif/dot_general | solution.py:43
  72.1 11.3 %copy.12 = f32[152,128,128]{2,1,0:T(8,128)} copy(f32[152,128,128]{1,2,0:T(8,128)} %fusion.4) | data formatting | bytes 19922944 | tf_op jit(solution)/shard_map/kij,kjf->kif/dot_general | solution.py:43
  83.5 0.2 broadcast_in_dim.17
  83.7 21.0 %scatter_fusion = f32[33,128,128]{2,1,0:T(8,128)S(1)} fusion(f32[33,128,128]{2,1,0:T(8,128)S(1)} %broadcast_in_dim.17, s32[152]{0:T(256)S(1)} %bitcast.51, f32[152,128,128]{2,1,0:T(8,128)} %copy.12), kind=kCustom, calls=%fused_computation.3 | custom fusion | flops 2490368 | bytes 29885024 | tf_op jit(solution)/shard_map/scatter-add | solution.py:24
  104.7 1.5 slice.14
  106.2 94.5 %reduce-scatter.3.cloned.1.call-done = f32[128,128]{1,0:T(8,128)} async-done(((f32[4096,128]{1,0:T(8,128)}), f32[128,128]{1,0:T(8,128)}) %reduce-scatter.3.cloned.1.call-update) | async-done | bytes 65552 | tf_op jit(solution)/shard_map/reduce_scatter | solution.py:47
  200.8 1.0 multiply_convert_fusion
  201.8 0.8 convolution_convert_fusion
  202.6 1.7 fusion.10
  204.3 0.2 reduce-scatter.5.cloned.1.call-start
  204.5 54.7 %all-gather.2.cloned.1.call-done = bf16[4096,128]{1,0:T(8,128)(2,1)} async-done(((bf16[128,128]{1,0:T(8,128)(2,1)}), bf16[4096,128]{1,0:T(8,128)(2,1)}) %all-gather.2.cloned.1.call-update) | async-done | bytes 1048592 | tf_op jit(solution)/shard_map/all_gather | solution.py:51
  259.3 8.9 %gather_fusion.1 = bf16[152,128,128]{2,1,0:T(8,128)(2,1)} fusion(bf16[32,128,128]{2,1,0:T(8,128)(2,1)} %bitcast.47, s32[1024]{0:T(1024)S(1)} %pad_clamp_fusion.1), kind=kCustom, calls=%fused_computation.1 | custom fusion | bytes 9962080 | tf_op jit(solution)/shard_map/gather | solution.py:53
  268.2 9.5 %fusion.7 = f32[152,128,128]{1,2,0:T(8,128)} fusion(bf16[152,128,128]{2,1,0:T(8,128)(2,1)} %gather_fusion.1, bf16[1,1,152,128,128]{4,3,2,1,0:T(8,128)(2,1)} %param.11), kind=kOutput, calls=%fused_computation.10 | convolution fusion | flops 637534208 | bytes 19922944 | tf_op jit(solution)/shard_map/kij,kif->kjf/dot_general | solution.py:54
  277.7 11.3 %copy.14 = f32[152,128,128]{2,1,0:T(8,128)} copy(f32[152,128,128]{1,2,0:T(8,128)} %fusion.7) | data formatting | bytes 19922944 | tf_op jit(solution)/shard_map/kij,kif->kjf/dot_general | solution.py:54
  289.2 21.0 %scatter_fusion.1 = f32[17,128,128]{2,1,0:T(8,128)S(1)} fusion(f32[17,128,128]{2,1,0:T(8,128)S(1)} %broadcast_in_dim.16, s32[152]{0:T(256)S(1)} %bitcast.50, f32[152,128,128]{2,1,0:T(8,128)} %copy.14), kind=kCustom, calls=%fused_computation.4 | custom fusion | flops 2490368 | bytes 29885024 | tf_op jit(solution)/shard_map/scatter-add | solution.py:24
  310.1 1.0 slice.15
  311.2 211.2 %all-reduce.2.cloned.1.call-done = f32[128,128]{1,0:T(8,128)} async-done(((f32[128,128]{1,0:T(8,128)}), f32[128,128]{1,0:T(8,128)}) %all-reduce.2.cloned.1.call-update) | async-done | bytes 65552 | tf_op jit(solution)/shard_map/psum | solution.py:52
  522.4 1.5 broadcast_multiply_fusion
  523.9 74.6 %reduce-scatter.5.cloned.1.call-done = f32[128,128]{1,0:T(8,128)} async-done(((f32[2048,128]{1,0:T(8,128)}), f32[128,128]{1,0:T(8,128)}) %reduce-scatter.5.cloned.1.call-update) | async-done | bytes 65552 | tf_op jit(solution)/shard_map/reduce_scatter | solution.py:60
  598.5 0.8 convert_element_type.19
  599.4 1.3 gather_fusion.2
  (19 shorter events, 0.3 us)
Async XLA Ops:
  7.2 193.6 %copy-start = (bf16[128,128]{1,0:T(8,128)(2,1)S(1)}, bf16[128,128]{1,0:T(8,128)(2,1)}, u32[]{:S(2)}) copy-start(bf16[128,128]{1,0:T(8,128)(2,1)} %param.9) | copy-start | bytes 98308
  7.2 193.6 %reduce-scatter.3.cloned.1.call-start = ((), (), s32[]{:S(2)}) async-start(), calls=%async_computation.2 | async-start | bytes 2162688 | tf_op jit(solution)/shard_map/reduce_scatter | solution.py:47
  104.7 96.1 %copy-start.1 = (bf16[128,128]{1,0:T(8,128)(2,1)S(1)}, bf16[128,128]{1,0:T(8,128)(2,1)}, u32[]{:S(2)}) copy-start(bf16[128,128]{1,0:T(8,128)(2,1)} %param.8) | copy-start | bytes 98308
  106.2 153.1 %all-gather.2.cloned.1.call-start = ((), (), s32[]{:S(2)}) async-start(), calls=%async_computation.3 | async-start | bytes 1081344 | tf_op jit(solution)/shard_map/all_gather | solution.py:51
  202.6 319.9 %all-reduce.2.cloned.1.call-start = ((), (), s32[]{:S(2)}) async-start(), calls=%async_computation.5 | async-start | bytes 131072 | tf_op jit(solution)/shard_map/psum | solution.py:52
  204.3 394.2 %reduce-scatter.5.cloned.1.call-start = ((), (), s32[]{:S(2)}) async-start(), calls=%async_computation.4 | async-start | bytes 1114112 | tf_op jit(solution)/shard_map/reduce_scatter | solution.py:60
  289.2 22.1 %copy-start.2 = (s32[1,128]{1,0:T(1,128)S(1)}, s32[1,128]{1,0:T(1,128)}, u32[]{:S(2)}) copy-start(s32[1,128]{1,0:T(1,128)} %param.13) | copy-start | bytes 1540
Sparse Core Ops, SparseCore 0:
  106.3 94.3 reduce-scatter.2
  204.5 54.7 all-gather.1
  264.8 257.5 all-reduce.1
  525.1 73.4 reduce-scatter.4
where the time goes:
time: 609 us; the launch traced here: 607 us
  waiting for transfers between devices  435 us (71%)
  other arithmetic  45 us (7%)
  blocking collectives  44.5 us (7%)
  local copies, waits for them, and re-layouts  43.5 us (7%)
  matrix products  24.3 us (4%)
  between operations  14.5 us (2%)
    psum x1, waiting for transfers between devices, shards(): lax.psum(weight_part, ('row', 'col')) * (1.0 / math.sqrt(total_nodes))  211 us
    reduce_scatter x1, waiting for transfers between devices, shards(): lax.psum_scatter(partial_value, 'col', scatter_dimension=0, tiled=True)  94.5 us
    reduce_scatter x1, waiting for transfers between devices, shards(): lax.psum_scatter(partial_back, 'row', scatter_dimension=0, tiled=True)  74.6 us
    all_gather x1, waiting for transfers between devices, shards(): grad_rows = lax.all_gather(grad_share, 'col', axis=0, tiled=True)  54.7 us
    all_gather x1, blocking collectives, shards(): column_source = lax.all_gather(features, 'row', axis=0, tiled=True)  44.5 us
    scatter-add x2, other arithmetic, block_sums(): summed = jax.ops.segment_sum(product, routed, num_segments=segments + 1)  41.9 us
  transfers between devices with their start and end apart: 4, of which 4 were waited for; matrix products, arithmetic and copies ran while one was open for 9% of the time, Pallas kernels for 0%

commit v1 on v0

--- a/solution.py
+++ b/solution.py
@@ -48,7 +48,9 @@
     agg_low = aggregate.astype(jnp.bfloat16)
     grad_pre, grad_share = grad_step(agg_low, grad_out, weight)
     weight_part = jnp.dot(agg_low.T, grad_pre, preferred_element_type=jnp.float32)
-    grad_rows = lax.all_gather(grad_share, "col", axis=0, tiled=True)
+    grad_rows = jnp.concatenate(
+        lax.all_to_all(jnp.stack([grad_share] * lax.axis_size("col")), "col", 0, 0), axis=0
+    )
     weight_grad = lax.psum(weight_part, ("row", "col")) * (1.0 / math.sqrt(total_nodes))
     picked_back = grad_rows.reshape(row_count, BLOCK, hidden)[block_row]
     product_back = jnp.einsum(

time: 609 us -> 563 us (0.924)
  waiting for transfers between devices: 435 us -> 383 us
  starting transfers between devices: 0.34 us -> 7.68 us
    all_gather x1 -> x0, waiting for transfers between devices: 54.7 us -> none  [shards(): grad_rows = lax.all_gather(grad_share, 'col', axis=0, tiled=True)]
    all_to_all x0 -> x1, waiting for transfers between devices: none -> 25.6 us  [shards(): lax.all_to_all(jnp.stack([grad_share] * lax.axis_size('col')), 'col', 0, 0)]
    psum x1, waiting for transfers between devices: 211 us -> 188 us  [shards(): lax.psum(weight_part, ('row', 'col')) * (1.0 / math.sqrt(total_nodes))]
    all_to_all x0 -> x1, starting transfers between devices: none -> 7.38 us  [shards(): lax.all_to_all(jnp.stack([grad_share] * lax.axis_size('col')), 'col', 0, 0)]
  transfers between devices with their start and end apart: 4 -> 4, of which waited for: 4 -> 4; matrix products, arithmetic and copies ran while one was open for 9% -> 10% of each run, Pallas kernels for 0% -> 0%
where the time goes in v1:
time: 563 us; the launch traced here: 562 us
  waiting for transfers between devices  383 us (68%)
  other arithmetic  45 us (8%)
  blocking collectives  44.5 us (8%)
  local copies, waits for them, and re-layouts  43.4 us (8%)
  matrix products  23.7 us (4%)
  between operations  14.5 us (3%)
  starting transfers between devices  7.68 us (1%)
    psum x1, waiting for transfers between devices, shards(): lax.psum(weight_part, ('row', 'col')) * (1.0 / math.sqrt(total_nodes))  188 us
    reduce_scatter x1, waiting for transfers between devices, shards(): lax.psum_scatter(partial_value, 'col', scatter_dimension=0, tiled=True)  94.6 us
    reduce_scatter x1, waiting for transfers between devices, shards(): lax.psum_scatter(partial_back, 'row', scatter_dimension=0, tiled=True)  74.8 us
    all_gather x1, blocking collectives, shards(): column_source = lax.all_gather(features, 'row', axis=0, tiled=True)  44.5 us
    scatter-add x2, other arithmetic, block_sums(): summed = jax.ops.segment_sum(product, routed, num_segments=segments + 1)  41.9 us
    all_to_all x1, waiting for transfers between devices, shards(): lax.all_to_all(jnp.stack([grad_share] * lax.axis_size('col')), 'col', 0, 0)  25.6 us
    dot_general x1, matrix products, shards(): jnp.einsum('kij,kjf->kif', values, picked, preferred_element_type=jnp.flo...  11.3 us
    dot_general x1, local copies, waits for them, and re-layouts, shards(): jnp.einsum('kij,kjf->kif', values, picked, preferred_element_type=jnp.flo...  11.3 us
  transfers between devices with their start and end apart: 4, of which 4 were waited for; matrix products, arithmetic and copies ran while one was open for 10% of the time, Pallas kernels for 0%

profile of v1, /device:TPU:4, one launch (start us, length us, event | category | flops | bytes accessed | tf_op | source)
XLA Modules:
  0.0 561.6 jit_solution(16592991521733176024)
XLA Ops:
  7.2 0.7 compare_select_fusion
  8.6 44.5 %all_gather.3 = bf16[2048,128]{1,0:T(8,128)(2,1)S(1)} all-gather(bf16[128,128]{1,0:T(8,128)(2,1)} %param.7), channel_id=1, replica_groups=mesh['row'=16,'col'=32] {'row'}, dimensions={0}, use_global_device_ids=true | all-gather | bytes 557056 | tf_op jit(solution)/shard_map/all_gather | solution.py:41
  53.1 7.7 %gather_fusion = bf16[152,128,128]{2,1,0:T(8,128)(2,1)} fusion(bf16[16,128,128]{2,1,0:T(8,128)(2,1)S(1)} %bitcast.45, s32[1024]{0:T(1024)S(1)} %pad_clamp_fusion.2), kind=kCustom, calls=%fused_computation | custom fusion | bytes 9962080 | tf_op jit(solution)/shard_map/gather | solution.py:42
  60.8 11.3 %fusion.4 = f32[152,128,128]{1,2,0:T(8,128)} fusion(bf16[152,128,128]{2,1,0:T(8,128)(2,1)} %gather_fusion, bf16[1,1,152,128,128]{4,3,2,1,0:T(8,128)(2,1)} %param.11), kind=kOutput, calls=%fused_computation.9 | convolution fusion | flops 637534208 | bytes 19922944 | tf_op jit(solution)/shard_map/kij,kjf->kif/dot_general | solution.py:43
  72.1 11.3 %copy.12 = f32[152,128,128]{2,1,0:T(8,128)} copy(f32[152,128,128]{1,2,0:T(8,128)} %fusion.4) | data formatting | bytes 19922944 | tf_op jit(solution)/shard_map/kij,kjf->kif/dot_general | solution.py:43
  83.4 0.2 broadcast_in_dim.17
  83.7 21.0 %scatter_fusion = f32[33,128,128]{2,1,0:T(8,128)S(1)} fusion(f32[33,128,128]{2,1,0:T(8,128)S(1)} %broadcast_in_dim.17, s32[152]{0:T(256)S(1)} %bitcast.49, f32[152,128,128]{2,1,0:T(8,128)} %copy.12), kind=kCustom, calls=%fused_computation.3 | custom fusion | flops 2490368 | bytes 29885024 | tf_op jit(solution)/shard_map/scatter-add | solution.py:24
  104.7 1.5 slice.14
  106.2 94.6 %reduce-scatter.3.cloned.1.call-done = f32[128,128]{1,0:T(8,128)} async-done(((f32[4096,128]{1,0:T(8,128)}), f32[128,128]{1,0:T(8,128)}) %reduce-scatter.3.cloned.1.call-update) | async-done | bytes 65552 | tf_op jit(solution)/shard_map/reduce_scatter | solution.py:47
  200.7 1.0 multiply_convert_fusion
  201.9 1.2 stack.2
  203.1 7.4 %all-to-all-start = ((bf16[32,128,128]{2,1,0:T(8,128)(2,1)}), bf16[32,128,128]{2,1,0:T(8,128)(2,1)S(1)}, u32[]{:S(2)}, u32[]{:S(2)}) async-start(bf16[32,128,128]{2,1,0:T(8,128)(2,1)} %stack.2), calls=%async_computation.1 | async-start | bytes 2097152 | tf_op jit(solution)/shard_map/all_to_all | solution.py:52
  210.6 1.7 fusion.10
  212.5 25.6 %all-to-all-done = bf16[32,128,128]{2,1,0:T(8,128)(2,1)S(1)} async-done(((bf16[32,128,128]{2,1,0:T(8,128)(2,1)}), bf16[32,128,128]{2,1,0:T(8,128)(2,1)S(1)}, u32[]{:S(2)}, u32[]{:S(2)}) %all-to-all-start) | async-done | bytes 1048608 | tf_op jit(solution)/shard_map/all_to_all | solution.py:52
  238.1 7.7 %gather_fusion.1 = bf16[152,128,128]{2,1,0:T(8,128)(2,1)} fusion(bf16[32,128,128]{2,1,0:T(8,128)(2,1)S(1)} %all-to-all-done, s32[1024]{0:T(1024)S(1)} %pad_clamp_fusion.1), kind=kCustom, calls=%fused_computation.1 | custom fusion | bytes 9962080 | tf_op jit(solution)/shard_map/gather | solution.py:55
  245.8 9.5 %fusion.7 = f32[152,128,128]{1,2,0:T(8,128)} fusion(bf16[152,128,128]{2,1,0:T(8,128)(2,1)} %gather_fusion.1, bf16[1,1,152,128,128]{4,3,2,1,0:T(8,128)(2,1)} %param.11), kind=kOutput, calls=%fused_computation.10 | convolution fusion | flops 637534208 | bytes 19922944 | tf_op jit(solution)/shard_map/kij,kif->kjf/dot_general | solution.py:56
  255.3 11.3 %copy.14 = f32[152,128,128]{2,1,0:T(8,128)} copy(f32[152,128,128]{1,2,0:T(8,128)} %fusion.7) | data formatting | bytes 19922944 | tf_op jit(solution)/shard_map/kij,kif->kjf/dot_general | solution.py:56
  266.8 21.0 %scatter_fusion.1 = f32[17,128,128]{2,1,0:T(8,128)S(1)} fusion(f32[17,128,128]{2,1,0:T(8,128)S(1)} %broadcast_in_dim.16, s32[152]{0:T(256)S(1)} %bitcast.48, f32[152,128,128]{2,1,0:T(8,128)} %copy.14), kind=kCustom, calls=%fused_computation.4 | custom fusion | flops 2490368 | bytes 29885024 | tf_op jit(solution)/shard_map/scatter-add | solution.py:24
  287.8 1.0 slice.15
  288.9 187.8 %all-reduce.2.cloned.1.call-done = f32[128,128]{1,0:T(8,128)} async-done(((f32[128,128]{1,0:T(8,128)}), f32[128,128]{1,0:T(8,128)}) %all-reduce.2.cloned.1.call-update) | async-done | bytes 65552 | tf_op jit(solution)/shard_map/psum | solution.py:54
  476.6 1.5 broadcast_multiply_fusion
  478.1 74.8 %reduce-scatter.5.cloned.1.call-done = f32[128,128]{1,0:T(8,128)} async-done(((f32[2048,128]{1,0:T(8,128)}), f32[128,128]{1,0:T(8,128)}) %reduce-scatter.5.cloned.1.call-update) | async-done | bytes 65552 | tf_op jit(solution)/shard_map/reduce_scatter | solution.py:62
  552.9 0.8 convert_element_type.19
  553.7 1.3 gather_fusion.2
  (19 shorter events, 0.6 us)
Async XLA Ops:
  7.2 193.6 %copy-start = (bf16[128,128]{1,0:T(8,128)(2,1)S(1)}, bf16[128,128]{1,0:T(8,128)(2,1)}, u32[]{:S(2)}) copy-start(bf16[128,128]{1,0:T(8,128)(2,1)} %param.9) | copy-start | bytes 98308
  7.2 193.6 %reduce-scatter.3.cloned.1.call-start = ((), (), s32[]{:S(2)}) async-start(), calls=%async_computation.3 | async-start | bytes 2162688 | tf_op jit(solution)/shard_map/reduce_scatter | solution.py:47
  104.7 96.1 %copy-start.1 = (bf16[128,128]{1,0:T(8,128)(2,1)S(1)}, bf16[128,128]{1,0:T(8,128)(2,1)}, u32[]{:S(2)}) copy-start(bf16[128,128]{1,0:T(8,128)(2,1)} %param.8) | copy-start | bytes 98308
  203.1 35.0 %all-to-all-start = ((bf16[32,128,128]{2,1,0:T(8,128)(2,1)}), bf16[32,128,128]{2,1,0:T(8,128)(2,1)S(1)}, u32[]{:S(2)}, u32[]{:S(2)}) async-start(bf16[32,128,128]{2,1,0:T(8,128)(2,1)} %stack.2), calls=%async_computation.1 | async-start | bytes 2097152 | tf_op jit(solution)/shard_map/all_to_all | solution.py:52
  210.5 266.1 %all-reduce.2.cloned.1.call-start = ((), (), s32[]{:S(2)}) async-start(), calls=%async_computation.5 | async-start | bytes 131072 | tf_op jit(solution)/shard_map/psum | solution.py:54
  212.3 340.6 %reduce-scatter.5.cloned.1.call-start = ((), (), s32[]{:S(2)}) async-start(), calls=%async_computation.4 | async-start | bytes 1114112 | tf_op jit(solution)/shard_map/reduce_scatter | solution.py:62
  266.8 22.1 %copy-start.2 = (s32[1,128]{1,0:T(1,128)S(1)}, s32[1,128]{1,0:T(1,128)}, u32[]{:S(2)}) copy-start(s32[1,128]{1,0:T(1,128)} %param.13) | copy-start | bytes 1540
Sparse Core Ops, SparseCore 0:
  106.3 94.3 reduce-scatter.2
  216.9 259.6 all-reduce.1
  479.4 73.4 reduce-scatter.4
